TPU v7x, 256 devices: a whole 4x4x8 slice. The times are simulated.
256 devices in a mesh: context: 16 (over z, core), heads: 16 (over x, y).
Axes of the slice: x: 4, y: 4, z: 8, core: 2. Of those that a mesh axis runs over, the one named last changes fastest.
Arguments:
- main_query: bfloat16 [256, 128, 576], P('context', 'heads'), may hold values from -6 to 6
- latent_keys: bfloat16 [32768, 576], P('context'), may hold values from -6 to 6
- head_lse: float32 [256, 128], P(None, 'heads'), may hold values from 4 to 8
- lengths: int32 [256], replicated, may hold values from 1 to 32768, as said below
- index_query: bfloat16 [256, 64, 128], P('heads'), may hold values from -256 to 256
- index_key: bfloat16 [32768, 128], P('context'), may hold values from -8 to 8
- index_weight: float32 [256, 64], P('heads'), may hold values from -2.4 to 2.4
Outputs:
- grad_index_query: float32 [256, 64, 128], P('heads', 'context')
- grad_index_key: float32 [32768, 128], P(('context', 'heads'))
Inputs may be any that keep to these rules, and one draw needn't show every extreme that they name: Query rows come in blocks of 16 consecutive rows whose lengths rise by one from row to row; some block ends at the last key.
All inputs are finite; a program needn't handle non-finite values.
Results may differ from a plain program's by a relative error of at most 0.0029.
Values may be sent and summed in bfloat16 or wider, within the bound.
A program may use at most 64 MiB of HBM per device.

v0:
```python
import math
import jax
import jax.numpy as jnp
from jax import lax
from jax.sharding import PartitionSpec as P

main_scale = 192.0 ** (-0.5)
loss_scale = 64.0
masked_low = -1e30


def head_mass(queries, lse_rows, len_rows, latent, first_key):
    row_count = queries.shape[0]
    block_rows = math.gcd(row_count, 64)
    steps_count = row_count // block_rows
    key_pos = first_key + jnp.arange(latent.shape[0], dtype=jnp.int32)

    def one_block(inputs):
        query_block, lse_block, len_block = inputs
        scores = (
            jnp.einsum("rhd,sd->rhs", query_block, latent, preferred_element_type=jnp.float32)
            * main_scale
        )
        summed = jnp.sum(jnp.exp(scores - lse_block[:, :, None]), axis=1)
        return jnp.where(key_pos[None, :] < len_block[:, None], summed, 0.0)

    stacked = lax.map(
        one_block,
        (
            queries.reshape((steps_count, block_rows) + queries.shape[1:]),
            lse_rows.reshape(steps_count, block_rows, lse_rows.shape[1]),
            len_rows.reshape(steps_count, block_rows),
        ),
    )
    return stacked.reshape(row_count, latent.shape[0])


def on_device(main_query, latent_keys, head_lse, lengths, index_query, index_key, index_weight):
    key_count = latent_keys.shape[0]
    first_key = lax.axis_index("context") * key_count
    own_rows = index_query.shape[0]
    row_first = lax.axis_index("heads") * own_rows
    partial_mass = head_mass(
        lax.all_gather(main_query, "context", axis=0, tiled=True),
        head_lse,
        lengths,
        latent_keys,
        first_key,
    )
    summed_mass = lax.psum(partial_mass, "heads")
    row_mass = lax.dynamic_slice_in_dim(summed_mass, row_first, own_rows, 0)
    own_len = lax.dynamic_slice_in_dim(lengths, row_first, own_rows, 0)
    visible = (first_key + jnp.arange(key_count, dtype=jnp.int32))[None, :] < own_len[:, None]
    heads_count = index_query.shape[1]
    width = index_query.shape[2]
    index_scale = width ** (-0.5)
    flat_query = index_query.reshape(own_rows * heads_count, width)
    block_keys = math.gcd(key_count, 512)
    block_total = key_count // block_keys
    key_blocks = index_key.reshape(block_total, block_keys, width)

    def block_dots(key_block):
        products = lax.dot_general(
            flat_query, key_block, (((1,), (1,)), ((), ())), preferred_element_type=jnp.float32
        )
        return products.reshape(own_rows, heads_count, key_block.shape[0])

    def block_logits(key_block):
        return (
            jnp.einsum(
                "tj,tjs->ts",
                index_weight,
                jax.nn.relu(block_dots(key_block)),
                precision=lax.Precision.HIGHEST,
            )
            * index_scale
        )

    logits = jnp.moveaxis(lax.map(block_logits, key_blocks), 0, 1).reshape(own_rows, key_count)
    local_top = jnp.max(jnp.where(visible, logits, masked_low), axis=1)
    mass_local = jnp.sum(row_mass, axis=1)
    top = lax.pmax(local_top, "context")
    weights_exp = jnp.where(visible, jnp.exp(logits - top[:, None]), 0.0)
    share_sum, mass_total = lax.psum((jnp.sum(weights_exp, axis=1), mass_local), "context")
    probability = weights_exp / share_sum[:, None]
    target = row_mass / mass_total[:, None]
    slopes = loss_scale * (probability - target)
    slope_blocks = slopes.reshape(own_rows, block_total, block_keys).transpose(1, 0, 2)

    def back_step(query_grad, inputs):
        key_block, slope_block = inputs
        products = block_dots(key_block)
        terms = jnp.where(
            products > 0, slope_block[:, None, :] * index_weight[:, :, None] * index_scale, 0.0
        )
        terms = terms.astype(jnp.bfloat16).reshape(own_rows * heads_count, key_block.shape[0])
        query_grad = query_grad + jnp.dot(terms, key_block, preferred_element_type=jnp.float32)
        key_grad = lax.dot_general(
            terms, flat_query, (((0,), (0,)), ((), ())), preferred_element_type=jnp.float32
        )
        return (query_grad, key_grad)

    start_grad = jnp.zeros((own_rows * heads_count, width), jnp.float32)
    query_grad, key_grads = lax.scan(back_step, start_grad, (key_blocks, slope_blocks))
    query_grad = query_grad.reshape(own_rows, heads_count, width)
    key_grad = key_grads.reshape(key_count, width)
    out_query = lax.psum_scatter(query_grad, "context", scatter_dimension=1, tiled=True)
    out_key = lax.psum_scatter(key_grad, "heads", scatter_dimension=0, tiled=True)
    return (out_query, out_key)


def solution(mesh):
    placed = (
        P("context", "heads", None),
        P("context", None),
        P(None, "heads"),
        P(),
        P("heads", None, None),
        P("context", None),
        P("heads", None),
    )
    return jax.shard_map(
        on_device,
        mesh=mesh,
        in_specs=placed,
        out_specs=(P("heads", "context", None), P(("context", "heads"), None)),
        check_vma=False,
    )
```

profile of v0, /device:TPU:2, one launch (start us, length us, event | category | flops | bytes accessed | tf_op | source)
XLA Modules:
  0.0 374.9 jit_solution(15053279912884742428)
XLA Ops:
  7.2 0.7 all-gather.2.cloned.1.call-update
  8.0 0.8 reshape.139
  8.8 0.8 dynamic_slice.31
  9.5 0.8 copy.25
  10.3 0.8 mul.63
  11.1 41.8 %all-gather.2.cloned.1.call-done = bf16[256,8,576]{2,1,0:T(8,128)(2,1)} async-done(((bf16[16,8,576]{2,1,0:T(8,128)(2,1)}), bf16[256,8,576]{2,1,0:T(8,128)(2,1)}) %all-gather.2.cloned.1.call-update) | async-done | bytes 2359312 | tf_op jit(solution)/shard_map/all_gather | solution.py:44
  52.9 22.9 %while.36 = (s32[]{:T(128)}, f32[4,64,2048]{2,1,0:T(8,128)}, s32[4,64]{1,0:T(4,128)S(1)}, bf16[4,64,8,576]{3,2,1,0:T(8,128)(2,1)}, bf16[2048,576]{0,1:T(8,128)(2...) while((s32[]{:T(128)}, f32[4,64,2048]{2,1,0:T(8,128)}, s32[4,64]{1,0:T(4,128)S(1)}, ...), condition=%wide.region_8.9_spmd.clone, body=%wide.region_6.8_spmd.clone.sunk | while | flops 1211238400 | bytes 4611937 | solution.py:27
  52.9 4.8 %exponential_reduce_fusion.2 = f32[64,2048]{1,0:T(8,128)S(1)} fusion(bf16[2048,576]{0,1:T(8,128)(2,1)} %get-tuple-element.382, f32[64,8]{1,0:T(8,128)S(1)} %dynamic-slice_bitcast_fusion.5, bf16[4,64,8,576]{3,2,1,0:T(8,128)(2,1)} %get-tuple-element.381, s32[]{:T(128)} %get-tuple-element.370), kind=kOutput, calls=%fused_computation.7.clone.1 | convolution fusion | flops 1210974208 | bytes 3541504 | tf_op jit(solution)/shard_map/while/body/eval_jaxpr/rhd,sd->rhs/dot_general | solution.py:21
  57.7 0.9 fusion.60
  58.6 4.8 %exponential_reduce_fusion.2 = f32[64,2048]{1,0:T(8,128)S(1)} fusion(bf16[2048,576]{0,1:T(8,128)(2,1)} %get-tuple-element.382, f32[64,8]{1,0:T(8,128)S(1)} %dynamic-slice_bitcast_fusion.5, bf16[4,64,8,576]{3,2,1,0:T(8,128)(2,1)} %get-tuple-element.381, s32[]{:T(128)} %get-tuple-element.370), kind=kOutput, calls=%fused_computation.7.clone.1 | convolution fusion | flops 1210974208 | bytes 3541504 | tf_op jit(solution)/shard_map/while/body/eval_jaxpr/rhd,sd->rhs/dot_general | solution.py:21
  63.4 0.9 fusion.60
  64.3 4.8 %exponential_reduce_fusion.2 = f32[64,2048]{1,0:T(8,128)S(1)} fusion(bf16[2048,576]{0,1:T(8,128)(2,1)} %get-tuple-element.382, f32[64,8]{1,0:T(8,128)S(1)} %dynamic-slice_bitcast_fusion.5, bf16[4,64,8,576]{3,2,1,0:T(8,128)(2,1)} %get-tuple-element.381, s32[]{:T(128)} %get-tuple-element.370), kind=kOutput, calls=%fused_computation.7.clone.1 | convolution fusion | flops 1210974208 | bytes 3541504 | tf_op jit(solution)/shard_map/while/body/eval_jaxpr/rhd,sd->rhs/dot_general | solution.py:21
  69.1 0.9 fusion.60
  70.0 4.8 %exponential_reduce_fusion.2 = f32[64,2048]{1,0:T(8,128)S(1)} fusion(bf16[2048,576]{0,1:T(8,128)(2,1)} %get-tuple-element.382, f32[64,8]{1,0:T(8,128)S(1)} %dynamic-slice_bitcast_fusion.5, bf16[4,64,8,576]{3,2,1,0:T(8,128)(2,1)} %get-tuple-element.381, s32[]{:T(128)} %get-tuple-element.370), kind=kOutput, calls=%fused_computation.7.clone.1 | convolution fusion | flops 1210974208 | bytes 3541504 | tf_op jit(solution)/shard_map/while/body/eval_jaxpr/rhd,sd->rhs/dot_general | solution.py:21
  74.8 0.9 fusion.60
  75.8 0.9 copy-done
  76.9 19.8 %while.35 = (s32[]{:T(128)}, f32[4,16,512]{2,1,0:T(8,128)S(1)}, bf16[4,512,128]{2,1,0:T(8,128)(2,1)S(1)}, bf16[1024,128]{1,0:T(8,128)(2,1)S(1)}, f32[16,64]{1,0:T(8,128)S(1)}, /*index=5*/s32[]{:T(128)}) while((s32[]{:T(128)}, f32[4,16,512]{2,1,0:T(8,128)S(1)}, bf16[4,512,128]{2,1,0:T(8,128)(2,1)S(1)}, bf16[1024,128]{1,0:T(8,128)(2,1)S(1)}, ...), condition=%wide.region_1.2_spmd, body=%wide.region_0.1_spmd.sunk | while | flops 141041664 | bytes 8884301 | solution.py:79
  76.9 1.8 maximum_bitcast_fusion.2
  78.7 1.9 copy.41
  80.6 1.2 fusion.56
  81.8 1.8 maximum_bitcast_fusion.2
  83.6 1.9 copy.41
  85.6 1.2 fusion.56
  86.8 1.8 maximum_bitcast_fusion.2
  88.6 1.9 copy.41
  90.5 1.2 fusion.56
  91.8 1.8 maximum_bitcast_fusion.2
  93.6 1.9 copy.41
  95.5 1.2 fusion.56
  97.0 24.9 %pmax.7 = f32[16]{0:T(128)S(1)} all-reduce(f32[16]{0:T(128)S(1)} %fusion.18), channel_id=1, replica_groups=mesh['context'=16,'heads'=16] {'context'}, use_global_device_ids=true, to_apply=%region_3.4 | all-reduce | flops 16 | bytes 128 | tf_op jit(solution)/shard_map/pmax | solution.py:82
  122.1 53.3 %all-reduce.3.cloned.1.call-done = f32[256,2048]{1,0:T(8,128)} async-done(((f32[256,2048]{1,0:T(8,128)}), f32[256,2048]{1,0:T(8,128)}) %all-reduce.3.cloned.1.call-update) | async-done | bytes 2097168 | tf_op jit(solution)/shard_map/psum | solution.py:50
  175.4 1.0 dynamic-slice_reduce_fusion
  176.4 24.2 %all-reduce = (f32[16]{0:T(128)S(1)}, f32[16]{0:T(128)S(1)}) all-reduce(f32[16]{0:T(128)S(1)} %dynamic-slice_reduce_fusion, f32[16]{0:T(128)S(1)} %fusion.19), channel_id=1, replica_groups=mesh['context'=16,'heads'=16] {'context'}, use_global_device_ids=true, to_apply=%region_11.12 | all-reduce | flops 32 | bytes 256 | tf_op jit(solution)/shard_map/psum | solution.py:84
  200.6 1.0 subtract_multiply_fusion
  201.6 0.7 copy.35
  202.3 26.9 %while.37 = (s32[]{:T(128)}, f32[1024,128]{1,0:T(8,128)S(1)}, f32[4,512,128]{2,1,0:T(8,128)}, bf16[4,512,128]{2,1,0:T(8,128)(2,1)S(1)}, bf16[1024,128]{1,0:T(8,1...) while((s32[]{:T(128)}, f32[1024,128]{1,0:T(8,128)S(1)}, ...), condition=%wide.wide.region_13.14_spmd.clone, body=%wide.wide.region_12.13_spmd.clone.sunk | while | flops 405536768 | bytes 13734523 | solution.py:104
  202.3 0.8 dynamic-slice_bitcast_fusion.6
  203.1 0.2 mul.80
  203.3 1.8 copy.42
  205.2 2.1 select_convert_fusion.3
  207.3 0.6 convolution_add_fusion.3
  207.9 1.1 fusion.67
  209.0 0.8 dynamic-slice_bitcast_fusion.6
  209.8 0.2 mul.80
  210.0 1.8 copy.42
  211.9 2.1 select_convert_fusion.3
  214.0 0.6 convolution_add_fusion.3
  214.6 1.1 fusion.67
  215.8 0.8 dynamic-slice_bitcast_fusion.6
  216.5 0.2 mul.80
  216.8 1.8 copy.42
  218.6 2.1 select_convert_fusion.3
  220.7 0.6 convolution_add_fusion.3
  221.3 1.1 fusion.67
  222.5 0.8 dynamic-slice_bitcast_fusion.6
  223.5 1.8 copy.42
  225.3 2.1 select_convert_fusion.3
  227.4 0.6 convolution_add_fusion.3
  228.1 1.2 fusion.67
  229.2 1.1 copy.27
  230.4 0.5 reduce-scatter.5.cloned.1.call-update
  231.0 56.1 %reduce-scatter.3.cloned.1.call-done = f32[16,4,128]{2,0,1:T(8,128)} async-done(((f32[16,64,128]{2,0,1:T(8,128)}), f32[16,4,128]{2,0,1:T(8,128)}) %reduce-scatter.3.cloned.1.call-update) | async-done | bytes 32784 | tf_op jit(solution)/shard_map/reduce_scatter | solution.py:107
  287.1 1.4 copy.28
  288.5 79.9 %reduce-scatter.5.cloned.1.call-done = f32[128,128]{1,0:T(8,128)} async-done(((f32[2048,128]{1,0:T(8,128)}), f32[128,128]{1,0:T(8,128)}) %reduce-scatter.5.cloned.1.call-update) | async-done | bytes 65552 | tf_op jit(solution)/shard_map/reduce_scatter | solution.py:108
  (37 shorter events, 1.2 us)
Async XLA Ops:
  7.2 45.7 %all-gather.2.cloned.1.call-start = ((), (), s32[]{:S(2)}) async-start(), calls=%async_computation.2 | async-start | bytes 2785280 | tf_op jit(solution)/shard_map/all_gather | solution.py:44
  7.9 167.5 %all-reduce.3.cloned.1.call-start = ((), (), s32[]{:S(2)}) async-start(), calls=%async_computation.3 | async-start | bytes 4194304 | tf_op jit(solution)/shard_map/psum | solution.py:50
  75.8 0.9 copy-start
  75.8 1.1 copy-start.1
  75.8 1.1 copy-start.2
  75.8 211.3 %reduce-scatter.3.cloned.1.call-start = ((), (), s32[]{:S(2)}) async-start(), calls=%async_computation.4 | async-start | bytes 557056 | tf_op jit(solution)/shard_map/reduce_scatter | solution.py:107
  230.4 138.0 %reduce-scatter.5.cloned.1.call-start = ((), (), s32[]{:S(2)}) async-start(), calls=%async_computation.5 | async-start | bytes 1114112 | tf_op jit(solution)/shard_map/reduce_scatter | solution.py:108
Sparse Core Ops, SparseCore 0:
  9.8 43.0 all-gather.1
  75.9 99.3 all-reduce.2
  230.5 56.5 reduce-scatter.2
  291.0 77.3 reduce-scatter.4
where the time goes:
time: 376 us; the launch traced here: 375 us
  waiting for transfers between devices  232 us (62%)
  blocking collectives  49.1 us (13%)
  matrix products  46.5 us (12%)
  local copies, waits for them, and re-layouts  26.4 us (7%)
  between operations  13.8 us (4%)
  other arithmetic  6.2 us (2%)
    reduce_scatter x1, waiting for transfers between devices, on_device(): lax.psum_scatter(key_grad, 'heads', scatter_dimension=0, tiled=True)  79.9 us
    reduce_scatter x1, waiting for transfers between devices, on_device(): lax.psum_scatter(query_grad, 'context', scatter_dimension=1, tiled=True)  56.1 us
    psum x1, waiting for transfers between devices, on_device(): summed_mass = lax.psum(partial_mass, 'heads')  53.3 us
    all_gather x1, waiting for transfers between devices, on_device(): lax.all_gather(main_query, 'context', axis=0, tiled=True)  41.8 us
    pmax x1, blocking collectives, on_device(): top = lax.pmax(local_top, 'context')  24.9 us
    psum x1, blocking collectives, on_device(): lax.psum((jnp.sum(weights_exp, axis=1), mass_local), 'context')  24.2 us
    dot_general x4, matrix products, one_block(): jnp.einsum('rhd,sd->rhs', query_block, latent, preferred_element_type=jnp...  19 us
    dot_general x8, matrix products, block_dots(): lax.dot_general(flat_query, key_block, (((1,), (1,)), ((), ())), preferre...  15.5 us
  transfers between devices with their start and end apart: 4, of which 4 were waited for; matrix products, arithmetic and copies ran while one was open for 7% of the time, Pallas kernels for 0%

commit v1 on v0

--- a/solution.py
+++ b/solution.py
@@ -47,7 +47,14 @@
         latent_keys,
         first_key,
     )
-    summed_mass = lax.psum(partial_mass, "heads")
+    n_slots = lax.axis_size("heads")
+    summed_mass, formed = (partial_mass, 0)
+    while 1 << formed < n_slots:
+        taken_in = lax.ppermute(
+            summed_mass, "heads", tuple(((dd, dd ^ 1 << formed) for dd in range(n_slots)))
+        )
+        summed_mass = summed_mass + taken_in
+        formed = formed + 1
     row_mass = lax.dynamic_slice_in_dim(summed_mass, row_first, own_rows, 0)
     own_len = lax.dynamic_slice_in_dim(lengths, row_first, own_rows, 0)
     visible = (first_key + jnp.arange(key_count, dtype=jnp.int32))[None, :] < own_len[:, None]

time: 376 us -> 462 us (1.23)
  waiting for transfers between devices: 232 us -> 318 us
  starting transfers between devices: 0.16 us -> 7.43 us
  local copies, waits for them, and re-layouts: 26.4 us -> 20.5 us
    ppermute x0 -> x4, waiting for transfers between devices: none -> 137 us  [on_device(): lax.ppermute(summed_mass, 'heads', tuple(((dd, dd ^ 1 << formed) for dd i...]
    psum x1 -> x0, waiting for transfers between devices: 53.3 us -> none  [on_device(): summed_mass = lax.psum(partial_mass, 'heads')]
    ppermute x0 -> x4, starting transfers between devices: none -> 7.31 us  [on_device(): lax.ppermute(summed_mass, 'heads', tuple(((dd, dd ^ 1 << formed) for dd i...]
  transfers between devices with their start and end apart: 4 -> 7, of which waited for: 4 -> 7; matrix products, arithmetic and copies ran while one was open for 7% -> 5% of each run, Pallas kernels for 0% -> 0%
where the time goes in v1:
time: 462 us; the launch traced here: 461 us
  waiting for transfers between devices  318 us (69%)
  blocking collectives  48.1 us (10%)
  matrix products  46.4 us (10%)
  local copies, waits for them, and re-layouts  20.5 us (4%)
  between operations  13.8 us (3%)
  starting transfers between devices  7.43 us (2%)
  other arithmetic  6.96 us (2%)
    ppermute x4, waiting for transfers between devices, on_device(): lax.ppermute(summed_mass, 'heads', tuple(((dd, dd ^ 1 << formed) for dd i...  137 us
    reduce_scatter x1, waiting for transfers between devices, on_device(): lax.psum_scatter(key_grad, 'heads', scatter_dimension=0, tiled=True)  80 us
    reduce_scatter x1, waiting for transfers between devices, on_device(): lax.psum_scatter(query_grad, 'context', scatter_dimension=1, tiled=True)  55.3 us
    all_gather x1, waiting for transfers between devices, on_device(): lax.all_gather(main_query, 'context', axis=0, tiled=True)  43.3 us
    pmax x1, blocking collectives, on_device(): top = lax.pmax(local_top, 'context')  24.5 us
    psum x1, blocking collectives, on_device(): lax.psum((jnp.sum(weights_exp, axis=1), mass_local), 'context')  23.5 us
    dot_general x4, matrix products, one_block(): jnp.einsum('rhd,sd->rhs', query_block, latent, preferred_element_type=jnp...  19 us
    dot_general x8, matrix products, block_dots(): lax.dot_general(flat_query, key_block, (((1,), (1,)), ((), ())), preferre...  15.4 us
  transfers between devices with their start and end apart: 7, of which 7 were waited for; matrix products, arithmetic and copies ran while one was open for 5% of the time, Pallas kernels for 0%

profile of v1, /device:TPU:2, one launch (start us, length us, event | category | flops | bytes accessed | tf_op | source)
XLA Modules:
  0.0 461.2 jit_solution(17442033110339471409)
XLA Ops:
  7.2 0.7 all-gather.2.cloned.1.call-update
  8.0 0.8 copy.26
  8.8 0.8 reshape.139
  9.6 43.3 %all-gather.2.cloned.1.call-done = bf16[256,8,576]{2,1,0:T(8,128)(2,1)} async-done(((bf16[16,8,576]{2,1,0:T(8,128)(2,1)}), bf16[256,8,576]{2,1,0:T(8,128)(2,1)}) %all-gather.2.cloned.1.call-update) | async-done | bytes 2359312 | tf_op jit(solution)/shard_map/all_gather | solution.py:44
  52.9 19.7 %while.36 = (s32[]{:T(128)}, f32[4,64,2048]{2,1,0:T(8,128)S(1)}, s32[4,64]{1,0:T(4,128)S(1)}, bf16[4,64,8,576]{3,2,1,0:T(8,128)(2,1)}, bf16[2048,576]{0,1:T(8,12...) while((s32[]{:T(128)}, f32[4,64,2048]{2,1,0:T(8,128)S(1)}, s32[4,64]{1,0:T(4,128)S(1)}, ...), condition=%wide.region_8.9_spmd.clone, body=%wide.region_6.8_spmd.clone.sunk | while | flops 1211238400 | bytes 4611685 | solution.py:27
  52.9 4.8 %exponential_reduce_fusion.2 = f32[64,2048]{1,0:T(8,128)S(1)} fusion(bf16[2048,576]{0,1:T(8,128)(2,1)} %get-tuple-element.382, f32[64,8]{1,0:T(8,128)S(1)} %dynamic-slice_bitcast_fusion.5, bf16[4,64,8,576]{3,2,1,0:T(8,128)(2,1)} %get-tuple-element.381, s32[]{:T(128)} %get-tuple-element.370), kind=kOutput, calls=%fused_computation.7.clone.1 | convolution fusion | flops 1210974208 | bytes 3541504 | tf_op jit(solution)/shard_map/while/body/eval_jaxpr/rhd,sd->rhs/dot_general | solution.py:21
  57.8 4.8 %exponential_reduce_fusion.2 = f32[64,2048]{1,0:T(8,128)S(1)} fusion(bf16[2048,576]{0,1:T(8,128)(2,1)} %get-tuple-element.382, f32[64,8]{1,0:T(8,128)S(1)} %dynamic-slice_bitcast_fusion.5, bf16[4,64,8,576]{3,2,1,0:T(8,128)(2,1)} %get-tuple-element.381, s32[]{:T(128)} %get-tuple-element.370), kind=kOutput, calls=%fused_computation.7.clone.1 | convolution fusion | flops 1210974208 | bytes 3541504 | tf_op jit(solution)/shard_map/while/body/eval_jaxpr/rhd,sd->rhs/dot_general | solution.py:21
  62.8 4.8 %exponential_reduce_fusion.2 = f32[64,2048]{1,0:T(8,128)S(1)} fusion(bf16[2048,576]{0,1:T(8,128)(2,1)} %get-tuple-element.382, f32[64,8]{1,0:T(8,128)S(1)} %dynamic-slice_bitcast_fusion.5, bf16[4,64,8,576]{3,2,1,0:T(8,128)(2,1)} %get-tuple-element.381, s32[]{:T(128)} %get-tuple-element.370), kind=kOutput, calls=%fused_computation.7.clone.1 | convolution fusion | flops 1210974208 | bytes 3541504 | tf_op jit(solution)/shard_map/while/body/eval_jaxpr/rhd,sd->rhs/dot_general | solution.py:21
  67.7 4.8 %exponential_reduce_fusion.2 = f32[64,2048]{1,0:T(8,128)S(1)} fusion(bf16[2048,576]{0,1:T(8,128)(2,1)} %get-tuple-element.382, f32[64,8]{1,0:T(8,128)S(1)} %dynamic-slice_bitcast_fusion.5, bf16[4,64,8,576]{3,2,1,0:T(8,128)(2,1)} %get-tuple-element.381, s32[]{:T(128)} %get-tuple-element.370), kind=kOutput, calls=%fused_computation.7.clone.1 | convolution fusion | flops 1210974208 | bytes 3541504 | tf_op jit(solution)/shard_map/while/body/eval_jaxpr/rhd,sd->rhs/dot_general | solution.py:21
  72.6 1.6 collective-permute-start
  74.2 46.3 %collective-permute-done = f32[256,2048]{1,0:T(8,128)S(1)} collective-permute-done((f32[256,2048]{1,0:T(8,128)S(1)}, f32[256,2048]{1,0:T(8,128)S(1)}, u32[]{:S(2)}, u32[]{:S(2)}) %collective-permute-start) | collective-permute-done | bytes 2097184 | tf_op jit(solution)/shard_map/ppermute | solution.py:53
  120.5 0.3 bitcast_add_fusion
  120.8 3.1 collective-permute-start.1
  123.9 45.4 %collective-permute-done.1 = f32[256,2048]{1,0:T(8,128)S(1)} collective-permute-done((f32[256,2048]{1,0:T(8,128)S(1)}, f32[256,2048]{1,0:T(8,128)S(1)}, u32[]{:S(2)}, u32[]{:S(2)}) %collective-permute-start.1) | collective-permute-done | bytes 2097184 | tf_op jit(solution)/shard_map/ppermute | solution.py:53
  169.3 0.2 add.60
  169.6 0.6 collective-permute-start.2
  170.4 45.5 %collective-permute-done.2 = f32[256,2048]{1,0:T(8,128)} collective-permute-done((f32[256,2048]{1,0:T(8,128)S(1)}, f32[256,2048]{1,0:T(8,128)}, u32[]{:S(2)}, u32[]{:S(2)}) %collective-permute-start.2) | collective-permute-done | bytes 2097184 | tf_op jit(solution)/shard_map/ppermute | solution.py:53
  215.8 3.3 add.61
  219.1 2.0 collective-permute-start.3
  221.1 19.7 %while.35 = (s32[]{:T(128)}, f32[4,16,512]{2,1,0:T(8,128)S(1)}, bf16[4,512,128]{2,1,0:T(8,128)(2,1)S(1)}, bf16[1024,128]{1,0:T(8,128)(2,1)S(1)}, f32[16,64]{1,0:T(8,128)S(1)}, /*index=5*/s32[]{:T(128)}) while((s32[]{:T(128)}, f32[4,16,512]{2,1,0:T(8,128)S(1)}, bf16[4,512,128]{2,1,0:T(8,128)(2,1)S(1)}, bf16[1024,128]{1,0:T(8,128)(2,1)S(1)}, ...), condition=%wide.region_1.2_spmd, body=%wide.region_0.1_spmd.sunk | while | flops 141041664 | bytes 8884301 | solution.py:86
  221.1 1.8 maximum_bitcast_fusion.2
  222.9 1.9 copy.42
  224.8 1.2 fusion.57
  226.1 1.8 maximum_bitcast_fusion.2
  227.8 1.9 copy.42
  229.8 1.2 fusion.57
  231.0 1.8 maximum_bitcast_fusion.2
  232.8 1.9 copy.42
  234.7 1.2 fusion.57
  235.9 1.8 maximum_bitcast_fusion.2
  237.7 1.9 copy.42
  239.6 1.2 fusion.57
  241.1 24.5 %pmax.7 = f32[16]{0:T(128)S(1)} all-reduce(f32[16]{0:T(128)S(1)} %fusion.18), channel_id=1, replica_groups=mesh['context'=16,'heads'=16] {'context'}, use_global_device_ids=true, to_apply=%region_3.4 | all-reduce | flops 16 | bytes 128 | tf_op jit(solution)/shard_map/pmax | solution.py:89
  265.6 0.2 fusion.19
  265.8 0.3 collective-permute-done.3
  266.1 1.1 fusion.21
  267.2 23.5 %all-reduce = (f32[16]{0:T(128)S(1)}, f32[16]{0:T(128)S(1)}) all-reduce(f32[16]{0:T(128)S(1)} %fusion.21, f32[16]{0:T(128)S(1)} %fusion.19), channel_id=1, replica_groups=mesh['context'=16,'heads'=16] {'context'}, use_global_device_ids=true, to_apply=%region_10.11 | all-reduce | flops 32 | bytes 256 | tf_op jit(solution)/shard_map/psum | solution.py:91
  290.8 1.1 subtract_multiply_fusion
  291.9 24.2 %while.37 = (s32[]{:T(128)}, f32[1024,128]{1,0:T(8,128)S(1)}, f32[4,512,128]{2,1,0:T(8,128)}, bf16[4,512,128]{2,1,0:T(8,128)(2,1)S(1)}, bf16[1024,128]{1,0:T(8,1...) while((s32[]{:T(128)}, f32[1024,128]{1,0:T(8,128)S(1)}, ...), condition=%wide.wide.region_12.13_spmd.clone, body=%wide.wide.region_11.12_spmd.clone.sunk | while | flops 405536768 | bytes 13734523 | solution.py:111
  291.9 0.3 mul.80
  292.2 1.9 copy.43
  294.0 2.1 select_convert_fusion.3
  296.1 0.6 convolution_add_fusion.3
  296.8 1.2 fusion.68
  297.9 0.3 mul.80
  298.2 1.9 copy.43
  300.1 2.1 select_convert_fusion.3
  302.2 0.6 convolution_add_fusion.3
  302.8 1.1 fusion.68
  304.0 0.3 mul.80
  304.2 1.9 copy.43
  306.1 2.1 select_convert_fusion.3
  308.2 0.6 convolution_add_fusion.3
  308.9 1.2 fusion.68
  310.0 0.3 mul.80
  310.3 1.9 copy.43
  312.2 2.1 select_convert_fusion.3
  314.3 0.6 convolution_add_fusion.3
  314.9 1.2 fusion.68
  316.1 1.1 copy.28
  317.2 0.7 reduce-scatter.5.cloned.1.call-update
  317.9 55.3 %reduce-scatter.3.cloned.1.call-done = f32[16,4,128]{2,0,1:T(8,128)} async-done(((f32[16,64,128]{2,0,1:T(8,128)}), f32[16,4,128]{2,0,1:T(8,128)}) %reduce-scatter.3.cloned.1.call-update) | async-done | bytes 32784 | tf_op jit(solution)/shard_map/reduce_scatter | solution.py:114
  373.3 1.4 copy.29
  374.6 80.0 %reduce-scatter.5.cloned.1.call-done = f32[128,128]{1,0:T(8,128)} async-done(((f32[2048,128]{1,0:T(8,128)}), f32[128,128]{1,0:T(8,128)}) %reduce-scatter.5.cloned.1.call-update) | async-done | bytes 65552 | tf_op jit(solution)/shard_map/reduce_scatter | solution.py:115
  (47 shorter events, 1.1 us)
Async XLA Ops:
  7.2 45.7 %all-gather.2.cloned.1.call-start = ((), (), s32[]{:S(2)}) async-start(), calls=%async_computation.2 | async-start | bytes 2785280 | tf_op jit(solution)/shard_map/all_gather | solution.py:44
  7.9 365.4 %reduce-scatter.3.cloned.1.call-start = ((), (), s32[]{:S(2)}) async-start(), calls=%async_computation.3 | async-start | bytes 557056 | tf_op jit(solution)/shard_map/reduce_scatter | solution.py:114
  72.6 47.9 %collective-permute-start = (f32[256,2048]{1,0:T(8,128)S(1)}, f32[256,2048]{1,0:T(8,128)S(1)}, u32[]{:S(2)}, u32[]{:S(2)}) collective-permute-start(f32[256,2048]{1,0:T(8,128)S(1)} %bitcast.137), channel_id=1, source_target_pairs={{0,1},{1,0},{2,3},{3,2},{4,5},{5,4},{6,7},{7,6},{8,9},{9,8},{10,11... | collective-permute-start | bytes 6291464 | tf_op jit(solution)/shard_map/ppermute | solution.py:53
  120.8 49.4 %copy-start.3 = (s32[256]{0:T(256)S(1)}, s32[256]{0:T(256)}, u32[]{:S(2)}) copy-start(s32[256]{0:T(256)} %param.16) | copy-start | bytes 3076
  120.8 49.5 %copy-start.2 = (f32[16,64]{1,0:T(8,128)S(1)}, f32[16,64]{1,0:T(8,128)}, u32[]{:S(2)}) copy-start(f32[16,64]{1,0:T(8,128)} %param.19) | copy-start | bytes 12292
  120.8 48.5 %collective-permute-start.1 = (f32[256,2048]{1,0:T(8,128)S(1)}, f32[256,2048]{1,0:T(8,128)S(1)}, u32[]{:S(2)}, u32[]{:S(2)}) collective-permute-start(f32[256,2048]{1,0:T(8,128)S(1)} %bitcast_add_fusion), channel_id=1, source_target_pairs={{0,2},{1,3},{2,0},{3,1},{4,6},{5,7},{6,4},{7,5},{8,10},{9,11},{10,... | collective-permute-start | bytes 6291464 | tf_op jit(solution)/shard_map/ppermute | solution.py:53
  169.6 46.2 %collective-permute-start.2 = (f32[256,2048]{1,0:T(8,128)S(1)}, f32[256,2048]{1,0:T(8,128)}, u32[]{:S(2)}, u32[]{:S(2)}) collective-permute-start(f32[256,2048]{1,0:T(8,128)S(1)} %add.60), channel_id=1, source_target_pairs={{0,4},{1,5},{2,6},{3,7},{4,0},{5,1},{6,2},{7,3},{8,12},{9,13},{10,... | collective-permute-start | bytes 6291464 | tf_op jit(solution)/shard_map/ppermute | solution.py:53
  170.4 50.8 %copy-start = (bf16[16,64,128]{2,1,0:T(8,128)(2,1)S(1)}, bf16[16,64,128]{2,1,0:T(8,128)(2,1)}, u32[]{:S(2)}) copy-start(bf16[16,64,128]{2,1,0:T(8,128)(2,1)} %param.17) | copy-start | bytes 786436
  170.4 50.8 %copy-start.1 = (bf16[2048,128]{1,0:T(8,128)(2,1)S(1)}, bf16[2048,128]{1,0:T(8,128)(2,1)}, u32[]{:S(2)}) copy-start(bf16[2048,128]{1,0:T(8,128)(2,1)} %param.18) | copy-start | bytes 1572868
  219.1 47.0 %collective-permute-start.3 = (f32[256,2048]{1,0:T(8,128)}, f32[256,2048]{1,0:T(8,128)}, u32[]{:S(2)}, u32[]{:S(2)}) collective-permute-start(f32[256,2048]{1,0:T(8,128)} %add.61), channel_id=1, source_target_pairs={{0,8},{1,9},{2,10},{3,11},{4,12},{5,13},{6,14},{7,15},{8,0},{9,1},... | collective-permute-start | bytes 6291464 | tf_op jit(solution)/shard_map/ppermute | solution.py:53
  317.2 137.5 %reduce-scatter.5.cloned.1.call-start = ((), (), s32[]{:S(2)}) async-start(), calls=%async_computation.4 | async-start | bytes 1114112 | tf_op jit(solution)/shard_map/reduce_scatter | solution.py:115
Sparse Core Ops, SparseCore 0:
  9.8 43.0 all-gather.1
  317.3 55.9 reduce-scatter.2
  377.3 77.2 reduce-scatter.4
